TPU v7x, 32 devices: a whole 2x2x4 slice. The times are simulated.
32 devices in a mesh: lon: 8 (over y, x, core), bal: 4 (over z).
Axes of the slice: x: 2, y: 2, z: 4, core: 2. Of those that a mesh axis runs over, the one named last changes fastest.
Arguments:
- conc: float32 [65536, 128], P(('lon', 'bal')), may hold values from -6 to 6
- neighbours: int32 [512, 8], P(('lon', 'bal')), may hold values from 0 to 511, as said below
- counts: int32 [512], P(('lon', 'bal')), may hold values from 1 to 8
- weights: int32 [512, 8], P(('lon', 'bal')), may hold values from 1 to 15
- zones: int32 [65536], P(('lon', 'bal')), may hold values from 0 to 31
- owners: int32 [65536, 1], P(('lon', 'bal')), may hold values from 0 to 3; in each aligned block of 2048 rows (0 to 2047, 2048 to 4095, ...) at most 1024 rows name the same one
- rate_table: float32 [32, 128], replicated, may hold values from 0.05 to 1
- reaction: bfloat16 [128, 128], replicated, may hold values from -0.5 to 0.5
Outputs:
- conc_out: bfloat16 [65536, 128], P(('lon', 'bal'))
- chem_slots: bfloat16 [131072, 128], P(('lon', 'bal'))
Inputs may be any that keep to these rules, and one draw needn't show every extreme that they name: neighbours[g, k] is a block of the same bal index as g, on the same longitude band or on the band just before or after it, with the bands wrapping around. On every trajectory owner, at most 1024 of its parcels have the same owners value; on some trajectory owners one value is taken exactly 1024 times.
All inputs are finite; a program needn't handle non-finite values.
Results may differ from a plain program's by a relative error of at most 0.0085.
Values may be sent and summed in bfloat16 or wider, within the bound.
No kernel may reach another device: no remote copies, remote signals or barrier semaphores. Data moves between devices by JAX's collectives and lax.ppermute only.
A program may use at most 64 MiB of HBM per device.

v0:
```python
import jax
import jax.numpy as jnp
from jax import lax
from jax.sharding import PartitionSpec as P

BLK = 128
KADJ = 8
ZONES = 32
SUBSTEPS = 12


def extended_2(cells, sides, width):
    for axis, dim in sides:
        count = lax.axis_size(axis)
        head = lax.slice_in_dim(cells, 0, width, axis=dim)
        tail = lax.slice_in_dim(cells, cells.shape[dim] - width, cells.shape[dim], axis=dim)
        cells = jnp.concatenate(
            [
                lax.ppermute(tail, axis, [(i, (i + 1) % count) for i in range(count)]),
                cells,
                lax.ppermute(head, axis, [((i + 1) % count, i) for i in range(count)]),
            ],
            axis=dim,
        )
    return cells


def shifted(value, axis, steps):
    count = lax.axis_size(axis)
    pairs = [(source, (source + steps) % count) for source in range(count)]
    return lax.ppermute(value, axis, pairs)


def chemistry(state, reaction):

    def advance(step_index, current):
        tendency = jnp.dot(
            current.astype(jnp.bfloat16), reaction, preferred_element_type=jnp.float32
        )
        return current + 0.25 * jnp.tanh(tendency)

    return lax.fori_loop(0, SUBSTEPS, advance, state.astype(jnp.float32)).astype(jnp.bfloat16)


def shards(conc, neighbours, counts, weights, zones, owners, rate_table, reaction):
    rows, width = conc.shape
    nblocks = rows // BLK
    lon_count = lax.axis_size("lon")
    bal_count = lax.axis_size("bal")
    device_count = lon_count * bal_count
    self_device = lax.axis_index("lon") * bal_count + lax.axis_index("bal")
    own_blocks = conc.reshape(nblocks, BLK, width)
    extended = extended_2(own_blocks, (("lon", 0),), nblocks)
    used = jnp.arange(KADJ, dtype=jnp.int32)[None, :] < counts[:, None]
    coefs = jnp.where(used, weights.astype(jnp.float32) / 128.0, 0.0)
    local_part = neighbours % nblocks
    apart = (neighbours // nblocks - self_device + device_count) % device_count
    ext_index = (
        jnp.where(apart == 0, nblocks, jnp.where(apart == bal_count, 2 * nblocks, 0)) + local_part
    )
    change = jnp.zeros((nblocks, BLK, width), jnp.float32)
    sent = jnp.zeros((3 * nblocks, BLK, width), jnp.float32)
    for column in range(KADJ):
        flux = coefs[:, column][:, None, None] * (extended[ext_index[:, column]] - own_blocks)
        change = change + flux
        sent = sent.at[ext_index[:, column]].add(flux)
    from_right = shifted(sent[:nblocks].astype(jnp.bfloat16), "lon", -1).astype(jnp.float32)
    from_left = shifted(sent[2 * nblocks :].astype(jnp.bfloat16), "lon", 1).astype(jnp.float32)
    change = change - sent[nblocks : 2 * nblocks] - from_right - from_left
    mixed = (own_blocks + change).reshape(rows, width)
    zone_table = (zones[:, None] == jnp.arange(ZONES, dtype=jnp.int32)[None, :]).astype(jnp.float32)
    rates = jnp.dot(zone_table, rate_table, precision=lax.Precision.HIGHEST)
    moved = (mixed * jnp.exp(-rates)).astype(jnp.bfloat16)
    capacity = 2 * rows // bal_count
    owner = owners[:, 0]
    owner_table = (owner[:, None] == jnp.arange(bal_count, dtype=jnp.int32)[None, :]).astype(
        jnp.int32
    )
    rank = jnp.sum((jnp.cumsum(owner_table, axis=0) - owner_table) * owner_table, axis=1)
    slot = owner * capacity + rank
    conc_out = chemistry(moved, reaction)
    outgoing = jnp.zeros((bal_count * capacity, width), jnp.bfloat16).at[slot].set(conc_out)
    outgoing = outgoing.reshape(bal_count, capacity, width)
    chem_slots = lax.all_to_all(outgoing, "bal", split_axis=0, concat_axis=0, tiled=True).reshape(
        -1, width
    )
    return (conc_out, chem_slots)


def solution(mesh):
    in_specs = (
        P(("lon", "bal"), None),
        P(("lon", "bal"), None),
        P(("lon", "bal")),
        P(("lon", "bal"), None),
        P(("lon", "bal")),
        P(("lon", "bal"), None),
        P(),
        P(),
    )
    out_specs = (P(("lon", "bal"), None), P(("lon", "bal"), None))
    return jax.shard_map(shards, mesh=mesh, in_specs=in_specs, out_specs=out_specs, check_vma=False)
```

profile of v0, /device:TPU:0, one launch (start us, length us, event | category | flops | bytes accessed | tf_op | source)
XLA Modules:
  0.0 134.0 jit_solution(15365341471317218973)
XLA Ops:
  0.6 0.5 collective-permute-start
  1.2 2.9 %collective-permute-start.1 = (f32[16,128,128]{2,1,0:T(8,128)}, f32[16,128,128]{2,1,0:T(8,128)}, u32[]{:S(2)}, u32[]{:S(2)}) collective-permute-start(f32[16,128,128]{2,1,0:T(8,128)} %bitcast.69), channel_id=1, source_target_pairs={{4,0},{8,4},{12,8},{16,12},{20,16},{24,20},{28,24},{0,28},{5,1},{9... | collective-permute-start | bytes 3145736 | tf_op jit(solution)/shard_map/ppermute | solution.py:21
  4.1 0.7 fusion.19
  4.9 0.7 fusion.15
  5.6 1.1 reduce-window.6
  7.1 0.7 multiply_select_fusion
  7.9 17.5 %collective-permute-done = f32[16,128,128]{2,1,0:T(8,128)S(1)} collective-permute-done((f32[16,128,128]{2,1,0:T(8,128)}, f32[16,128,128]{2,1,0:T(8,128)S(1)}, u32[]{:S(2)}, u32[]{:S(2)}) %collective-permute-start) | collective-permute-done | bytes 1048608 | tf_op jit(solution)/shard_map/ppermute | solution.py:19
  25.4 1.0 copy-done.7
  26.4 0.6 collective-permute-done.1
  27.0 2.1 %pad_maximum_fusion = f32[48,128,128]{2,1,0:T(8,128)S(1)} fusion(f32[16,128,128]{2,1,0:T(8,128)} %collective-permute-done.1, f32[16,128,128]{2,1,0:T(8,128)} %bitcast.70, f32[16,128,128]{2,1,0:T(8,128)} %copy-done.7), kind=kLoop, calls=%fused_computation.21 | loop fusion | flops 1572864 | bytes 6291456 | tf_op jit(solution)/shard_map/concatenate | solution.py:17
  29.0 1.6 %gather_fusion = f32[16,128,128]{2,1,0:T(8,128)} fusion(f32[48,128,128]{2,1,0:T(8,128)S(1)} %pad_maximum_fusion, s32[1024]{0:T(1024)S(1)} %get-tuple-element.59), kind=kCustom, calls=%fused_computation | custom fusion | bytes 2097216 | tf_op jit(solution)/shard_map/gather | solution.py:64
  30.6 1.6 %gather_fusion.1 = f32[16,128,128]{2,1,0:T(8,128)} fusion(f32[48,128,128]{2,1,0:T(8,128)S(1)} %pad_maximum_fusion, s32[1024]{0:T(1024)S(1)} %get-tuple-element.58), kind=kCustom, calls=%fused_computation.1 | custom fusion | bytes 2097216 | tf_op jit(solution)/shard_map/gather | solution.py:64
  32.3 1.6 %gather_fusion.2 = f32[16,128,128]{2,1,0:T(8,128)} fusion(f32[48,128,128]{2,1,0:T(8,128)S(1)} %pad_maximum_fusion, s32[1024]{0:T(1024)S(1)} %get-tuple-element.57), kind=kCustom, calls=%fused_computation.2 | custom fusion | bytes 2097216 | tf_op jit(solution)/shard_map/gather | solution.py:64
  33.9 1.6 %gather_fusion.3 = f32[16,128,128]{2,1,0:T(8,128)} fusion(f32[48,128,128]{2,1,0:T(8,128)S(1)} %pad_maximum_fusion, s32[1024]{0:T(1024)S(1)} %get-tuple-element.56), kind=kCustom, calls=%fused_computation.3 | custom fusion | bytes 2097216 | tf_op jit(solution)/shard_map/gather | solution.py:64
  35.5 1.6 %gather_fusion.4 = f32[16,128,128]{2,1,0:T(8,128)} fusion(f32[48,128,128]{2,1,0:T(8,128)S(1)} %pad_maximum_fusion, s32[1024]{0:T(1024)S(1)} %get-tuple-element.55), kind=kCustom, calls=%fused_computation.4 | custom fusion | bytes 2097216 | tf_op jit(solution)/shard_map/gather | solution.py:64
  37.1 1.6 %gather_fusion.5 = f32[16,128,128]{2,1,0:T(8,128)} fusion(f32[48,128,128]{2,1,0:T(8,128)S(1)} %pad_maximum_fusion, s32[1024]{0:T(1024)S(1)} %get-tuple-element.54), kind=kCustom, calls=%fused_computation.5 | custom fusion | bytes 2097216 | tf_op jit(solution)/shard_map/gather | solution.py:64
  38.7 1.6 %gather_fusion.6 = f32[16,128,128]{2,1,0:T(8,128)} fusion(f32[48,128,128]{2,1,0:T(8,128)S(1)} %pad_maximum_fusion, s32[1024]{0:T(1024)S(1)} %get-tuple-element.53), kind=kCustom, calls=%fused_computation.6 | custom fusion | bytes 2097216 | tf_op jit(solution)/shard_map/gather | solution.py:64
  40.3 1.6 %gather_fusion.7 = f32[16,128,128]{2,1,0:T(8,128)} fusion(f32[48,128,128]{2,1,0:T(8,128)S(1)} %pad_maximum_fusion, s32[1024]{0:T(1024)S(1)} %get-tuple-element.52), kind=kCustom, calls=%fused_computation.7 | custom fusion | bytes 2097216 | tf_op jit(solution)/shard_map/gather | solution.py:64
  41.9 7.7 %subtract_multiply_fusion = (f32[16,128,128]{2,1,0:T(8,128)}, f32[16,128,128]{2,1,0:T(8,128)}, f32[16,128,128]{2,1,0:T(8,128)}, f32[16,128,128]{2,1,0:T(8,128)},...) fusion(f32[16,128,128]{2,1,0:T(8,128)} %gather_fusion.7, ...), kind=kLoop, calls=%fused_computation.31 | loop fusion | flops 4194304 | bytes 17826304 | tf_op jit(solution)/shard_map/mul | solution.py:64
  49.6 0.4 broadcast_in_dim.15
  50.0 2.6 %scatter_fusion = f32[48,128,128]{2,1,0:T(8,128)S(1)} fusion(f32[48,128,128]{2,1,0:T(8,128)S(1)} %broadcast_in_dim.15, s32[16]{0:T(128)S(1)} %get-tuple-element.51, f32[16,128,128]{2,1,0:T(8,128)} %get-tuple-element.35), kind=kCustom, calls=%fused_computation.8 | custom fusion | flops 262144 | bytes 3145792 | tf_op jit(solution)/shard_map/scatter-add | solution.py:66
  52.6 2.6 %scatter_fusion.1 = f32[48,128,128]{2,1,0:T(8,128)S(1)} fusion(f32[48,128,128]{2,1,0:T(8,128)S(1)} %scatter_fusion, s32[16]{0:T(128)S(1)} %get-tuple-element.50, f32[16,128,128]{2,1,0:T(8,128)} %get-tuple-element.34), kind=kCustom, calls=%fused_computation.9 | custom fusion | flops 262144 | bytes 3145792 | tf_op jit(solution)/shard_map/scatter-add | solution.py:66
  55.2 2.6 %scatter_fusion.2 = f32[48,128,128]{2,1,0:T(8,128)S(1)} fusion(f32[48,128,128]{2,1,0:T(8,128)S(1)} %scatter_fusion.1, s32[16]{0:T(128)S(1)} %get-tuple-element.49, f32[16,128,128]{2,1,0:T(8,128)} %get-tuple-element.33), kind=kCustom, calls=%fused_computation.10 | custom fusion | flops 262144 | bytes 3145792 | tf_op jit(solution)/shard_map/scatter-add | solution.py:66
  57.8 2.6 %scatter_fusion.3 = f32[48,128,128]{2,1,0:T(8,128)S(1)} fusion(f32[48,128,128]{2,1,0:T(8,128)S(1)} %scatter_fusion.2, s32[16]{0:T(128)S(1)} %get-tuple-element.48, f32[16,128,128]{2,1,0:T(8,128)} %get-tuple-element.32), kind=kCustom, calls=%fused_computation.11 | custom fusion | flops 262144 | bytes 3145792 | tf_op jit(solution)/shard_map/scatter-add | solution.py:66
  60.5 2.6 %scatter_fusion.4 = f32[48,128,128]{2,1,0:T(8,128)S(1)} fusion(f32[48,128,128]{2,1,0:T(8,128)S(1)} %scatter_fusion.3, s32[16]{0:T(128)S(1)} %get-tuple-element.47, f32[16,128,128]{2,1,0:T(8,128)} %get-tuple-element.31), kind=kCustom, calls=%fused_computation.12 | custom fusion | flops 262144 | bytes 3145792 | tf_op jit(solution)/shard_map/scatter-add | solution.py:66
  63.1 2.6 %scatter_fusion.5 = f32[48,128,128]{2,1,0:T(8,128)S(1)} fusion(f32[48,128,128]{2,1,0:T(8,128)S(1)} %scatter_fusion.4, s32[16]{0:T(128)S(1)} %get-tuple-element.46, f32[16,128,128]{2,1,0:T(8,128)} %get-tuple-element.30), kind=kCustom, calls=%fused_computation.13 | custom fusion | flops 262144 | bytes 3145792 | tf_op jit(solution)/shard_map/scatter-add | solution.py:66
  65.7 2.6 %scatter_fusion.6 = f32[48,128,128]{2,1,0:T(8,128)S(1)} fusion(f32[48,128,128]{2,1,0:T(8,128)S(1)} %scatter_fusion.5, s32[16]{0:T(128)S(1)} %get-tuple-element.45, f32[16,128,128]{2,1,0:T(8,128)} %get-tuple-element.29), kind=kCustom, calls=%fused_computation.14 | custom fusion | flops 262144 | bytes 3145792 | tf_op jit(solution)/shard_map/scatter-add | solution.py:66
  68.3 2.6 %scatter_fusion.7 = f32[48,128,128]{2,1,0:T(8,128)S(1)} fusion(f32[48,128,128]{2,1,0:T(8,128)S(1)} %scatter_fusion.6, s32[16]{0:T(128)S(1)} %get-tuple-element.44, f32[16,128,128]{2,1,0:T(8,128)} %get-tuple-element.28), kind=kCustom, calls=%fused_computation.15 | custom fusion | flops 262144 | bytes 3145792 | tf_op jit(solution)/shard_map/scatter-add | solution.py:66
  71.3 2.9 %collective-permute-start.2 = (bf16[16,128,128]{2,1,0:T(8,128)(2,1)S(1)}, bf16[16,128,128]{2,1,0:T(8,128)(2,1)S(1)}, u32[]{:S(2)}, u32[]{:S(2)}) collective-permute-start(bf16[16,128,128]{2,1,0:T(8,128)(2,1)S(1)} %get-tuple-element.26), channel_id=1, source_target_pairs={{0,28},{4,0},{8,4},{12,8},{16,12},{20,16},{24,20},{28,24},{1,29},{... | collective-permute-start | bytes 1572872 | tf_op jit(solution)/shard_map/ppermute | solution.py:31
  74.3 12.2 %collective-permute-done.2 = bf16[16,128,128]{2,1,0:T(8,128)(2,1)S(1)} collective-permute-done((bf16[16,128,128]{2,1,0:T(8,128)(2,1)S(1)}, bf16[16,128,128]{2,1,0:T(8,128)(2,1)S(1)}, u32[]{:S(2)}, u32[]{:S(2)}) %collective-permute-start.2) | collective-permute-done | bytes 524320 | tf_op jit(solution)/shard_map/ppermute | solution.py:31
  86.5 0.4 collective-permute-done.3
  87.0 3.1 %fusion.6 = f32[16,128,128]{2,1,0:T(8,128)S(1)} fusion(f32[16,128,128]{2,1,0:T(8,128)} %bitcast.72, f32[48,128,128]{2,1,0:T(8,128)S(1)} %scatter_fusion.7, bf16[16,128,128]{2,1,0:T(8,128)(2,1)S(1)} %collective-permute-done.3, bf16[16,128,128]{2,1,0:T(8,128)(2,1)S(1)} %collective-permute-done.2, f32[16,128,128]{2,1,0:T(8,128)S(1)} %copy-done.1, ...), kind=kLoop, calls=%fused_computation.27 | loop fusion | flops 3407872 | bytes 12582912 | tf_op jit(solution)/shard_map/add | solution.py:70
  90.1 1.1 fusion.8
  91.1 4.7 %while.10 = (s32[]{:T(128)}, f32[2048,128]{1,0:T(8,128)S(1)}, bf16[128,128]{1,0:T(8,128)(2,1)S(1)}, s32[]{:T(128)}) while((s32[]{:T(128)}, f32[2048,128]{1,0:T(8,128)S(1)}, bf16[128,128]{1,0:T(8,128)(2,1)S(1)}, s32[]{:T(128)}) %tuple.53), condition=%wide.region_9.10_spmd, body=%wide.region_8.9_spmd.sunk | while | flops 67895296 | bytes 4227125 | solution.py:42
  91.2 0.3 fusion.38
  91.6 0.3 fusion.38
  92.0 0.3 fusion.38
  92.8 0.3 fusion.38
  93.2 0.3 fusion.38
  93.9 0.3 fusion.38
  94.3 0.3 fusion.38
  95.1 0.3 fusion.38
  95.5 0.3 fusion.38
  95.8 6.8 %scatter_custom_fusion.8 = bf16[4096,128]{1,0:T(8,128)(2,1)} fusion(s32[2048]{0:T(1024)S(1)} %bitcast.77, bf16[]{:T(256)} %constant.76.clone.1, f32[2048,128]{1,0:T(8,128)S(1)} %get-tuple-element.19), kind=kCustom, calls=%fused_computation.40 | custom fusion | flops 262144 | bytes 2097154 | tf_op jit(solution)/shard_map/scatter | solution.py:82
  102.6 5.6 %all-to-all-start = ((bf16[4,1024,128]{2,1,0:T(8,128)(2,1)}), bf16[4,1024,128]{2,1,0:T(8,128)(2,1)S(1)}, u32[]{:S(2)}, u32[]{:S(2)}) async-start(bf16[4,1024,128]{2,1,0:T(8,128)(2,1)} %bitcast.23), calls=%async_computation | async-start | bytes 2097152 | tf_op jit(solution)/shard_map/all_to_all | solution.py:84
  108.2 0.8 convert_element_type.36
  109.1 24.0 %all-to-all-done = bf16[4,1024,128]{2,1,0:T(8,128)(2,1)S(1)} async-done(((bf16[4,1024,128]{2,1,0:T(8,128)(2,1)}), bf16[4,1024,128]{2,1,0:T(8,128)(2,1)S(1)}, u32[]{:S(2)}, u32[]{:S(2)}) %all-to-all-start) | async-done | bytes 1048608 | tf_op jit(solution)/shard_map/all_to_all | solution.py:84
  133.1 1.0 copy.30
  (50 shorter events, 2.6 us)
Async XLA Ops:
  0.6 89.4 %copy-start = (f32[32,128]{1,0:T(8,128)S(1)}, f32[32,128]{1,0:T(8,128)}, u32[]{:S(2)}) copy-start(f32[32,128]{1,0:T(8,128)} %param.16) | copy-start | bytes 49156
  0.6 24.8 %collective-permute-start = (f32[16,128,128]{2,1,0:T(8,128)}, f32[16,128,128]{2,1,0:T(8,128)S(1)}, u32[]{:S(2)}, u32[]{:S(2)}) collective-permute-start(f32[16,128,128]{2,1,0:T(8,128)} %bitcast.68), channel_id=1, source_target_pairs={{0,4},{4,8},{8,12},{12,16},{16,20},{20,24},{24,28},{28,0},{1,5},{5... | collective-permute-start | bytes 3145736 | tf_op jit(solution)/shard_map/ppermute | solution.py:19
  1.2 25.8 %collective-permute-start.1 = (f32[16,128,128]{2,1,0:T(8,128)}, f32[16,128,128]{2,1,0:T(8,128)}, u32[]{:S(2)}, u32[]{:S(2)}) collective-permute-start(f32[16,128,128]{2,1,0:T(8,128)} %bitcast.69), channel_id=1, source_target_pairs={{4,0},{8,4},{12,8},{16,12},{20,16},{24,20},{28,24},{0,28},{5,1},{9... | collective-permute-start | bytes 3145736 | tf_op jit(solution)/shard_map/ppermute | solution.py:21
  25.4 1.0 copy-start.7
  70.9 3.3 %copy-start.9 = (s32[2048,1]{0,1:T(1,128)S(1)}, s32[2048,1]{0,1:T(1,128)}, u32[]{:S(2)}) copy-start(s32[2048,1]{0,1:T(1,128)} %param.15) | copy-start | bytes 24580
  70.9 16.0 %copy-start.1 = (f32[16,128,128]{2,1,0:T(8,128)S(1)}, f32[16,128,128]{2,1,0:T(8,128)}, u32[]{:S(2)}) copy-start(f32[16,128,128]{2,1,0:T(8,128)} %get-tuple-element.28) | copy-start | bytes 3145732
  70.9 16.0 %copy-start.2 = (f32[16,128,128]{2,1,0:T(8,128)S(1)}, f32[16,128,128]{2,1,0:T(8,128)}, u32[]{:S(2)}) copy-start(f32[16,128,128]{2,1,0:T(8,128)} %get-tuple-element.29) | copy-start | bytes 3145732
  71.0 16.0 %copy-start.3 = (f32[16,128,128]{2,1,0:T(8,128)S(1)}, f32[16,128,128]{2,1,0:T(8,128)}, u32[]{:S(2)}) copy-start(f32[16,128,128]{2,1,0:T(8,128)} %get-tuple-element.30) | copy-start | bytes 3145732
  71.0 16.0 %copy-start.4 = (f32[16,128,128]{2,1,0:T(8,128)S(1)}, f32[16,128,128]{2,1,0:T(8,128)}, u32[]{:S(2)}) copy-start(f32[16,128,128]{2,1,0:T(8,128)} %get-tuple-element.31) | copy-start | bytes 3145732
  71.0 16.0 %copy-start.5 = (f32[16,128,128]{2,1,0:T(8,128)S(1)}, f32[16,128,128]{2,1,0:T(8,128)}, u32[]{:S(2)}) copy-start(f32[16,128,128]{2,1,0:T(8,128)} %get-tuple-element.32) | copy-start | bytes 3145732
  71.0 16.0 %copy-start.6 = (f32[16,128,128]{2,1,0:T(8,128)S(1)}, f32[16,128,128]{2,1,0:T(8,128)}, u32[]{:S(2)}) copy-start(f32[16,128,128]{2,1,0:T(8,128)} %get-tuple-element.33) | copy-start | bytes 3145732
  71.3 15.2 %collective-permute-start.2 = (bf16[16,128,128]{2,1,0:T(8,128)(2,1)S(1)}, bf16[16,128,128]{2,1,0:T(8,128)(2,1)S(1)}, u32[]{:S(2)}, u32[]{:S(2)}) collective-permute-start(bf16[16,128,128]{2,1,0:T(8,128)(2,1)S(1)} %get-tuple-element.26), channel_id=1, source_target_pairs={{0,28},{4,0},{8,4},{12,8},{16,12},{20,16},{24,20},{28,24},{1,29},{... | collective-permute-start | bytes 1572872 | tf_op jit(solution)/shard_map/ppermute | solution.py:31
  74.2 12.7 %collective-permute-start.3 = (bf16[16,128,128]{2,1,0:T(8,128)(2,1)S(1)}, bf16[16,128,128]{2,1,0:T(8,128)(2,1)S(1)}, u32[]{:S(2)}, u32[]{:S(2)}) collective-permute-start(bf16[16,128,128]{2,1,0:T(8,128)(2,1)S(1)} %get-tuple-element.27), channel_id=1, source_target_pairs={{0,4},{4,8},{8,12},{12,16},{16,20},{20,24},{24,28},{28,0},{1,5},{5... | collective-permute-start | bytes 1572872 | tf_op jit(solution)/shard_map/ppermute | solution.py:31
  74.3 15.8 %copy-start.10 = (s32[2048]{0:T(1024)S(1)}, s32[2048]{0:T(1024)}, u32[]{:S(2)}) copy-start(s32[2048]{0:T(1024)} %param.14) | copy-start | bytes 24580
  74.3 16.8 %copy-start.8 = (bf16[128,128]{1,0:T(8,128)(2,1)S(1)}, bf16[128,128]{1,0:T(8,128)(2,1)}, u32[]{:S(2)}) copy-start(bf16[128,128]{1,0:T(8,128)(2,1)} %param.17) | copy-start | bytes 98308
  102.6 30.5 %all-to-all-start = ((bf16[4,1024,128]{2,1,0:T(8,128)(2,1)}), bf16[4,1024,128]{2,1,0:T(8,128)(2,1)S(1)}, u32[]{:S(2)}, u32[]{:S(2)}) async-start(bf16[4,1024,128]{2,1,0:T(8,128)(2,1)} %bitcast.23), calls=%async_computation | async-start | bytes 2097152 | tf_op jit(solution)/shard_map/all_to_all | solution.py:84
where the time goes:
time: 135 us; the launch traced here: 134 us
  waiting for transfers between devices  54.7 us (41%)
  other arithmetic  45.2 us (33%)
  local copies, waits for them, and re-layouts  16.3 us (12%)
  starting transfers between devices  12 us (9%)
  matrix products  4.52 us (3%)
    all_to_all x1, waiting for transfers between devices, shards(): lax.all_to_all(outgoing, 'bal', split_axis=0, concat_axis=0, tiled=True)  24 us
    scatter-add x8, other arithmetic, shards(): sent = sent.at[ext_index[:, column]].add(flux)  20.9 us
    ppermute x1, waiting for transfers between devices, extended_2(): lax.ppermute(tail, axis, [(i, (i + 1) % count) for i in range(count)])  17.5 us
    gather x8, local copies, waits for them, and re-layouts, shards(): extended[ext_index[:, column]] - own_blocks  12.9 us
    ppermute x2, waiting for transfers between devices, shifted(): return lax.ppermute(value, axis, pairs)  12.6 us
    mul x1, other arithmetic, shards(): coefs[:, column][:, None, None]  7.75 us
    scatter x1, other arithmetic, shards(): jnp.zeros((bal_count * capacity, width), jnp.bfloat16).at[slot]  6.78 us
    all_to_all x1, starting transfers between devices, shards(): lax.all_to_all(outgoing, 'bal', split_axis=0, concat_axis=0, tiled=True)  5.63 us
  transfers between devices with their start and end apart: 5, of which 5 were waited for; matrix products, arithmetic and copies ran while one was open for 3% of the time, Pallas kernels for 0%

commit v1 on v0

--- a/solution.py
+++ b/solution.py
@@ -7,6 +7,37 @@
 KADJ = 8
 ZONES = 32
 SUBSTEPS = 12
+
+
+def change_vector(inner_x, ndim_at, xx):
+    t_next = inner_x.shape
+    tall = inner_x.reshape(*t_next[:ndim_at], xx, t_next[ndim_at] // xx, *t_next[ndim_at + 1 :])
+    o_now = jnp.moveaxis(tall, ndim_at, 0)
+    return o_now
+
+
+def matrix_time(target, where_dim):
+    target = jnp.moveaxis(target, 0, where_dim)
+    y1 = target.shape
+    y2 = target.reshape(*y1[:where_dim], y1[where_dim] * y1[where_dim + 1], *y1[where_dim + 2 :])
+    return y2
+
+
+def run_convert(here_x, mesh_dim, obj, in_array):
+    out_arr = lax.axis_size(mesh_dim)
+    state_next, vec_out = (out_arr, lax.axis_index(mesh_dim))
+    all_rows = change_vector(here_x, obj, state_next)
+    vals = [all_rows[vec_out]]
+    for b in range(1, state_next):
+        current_arr = all_rows[(vec_out + b) % state_next]
+        vals.append(
+            lax.ppermute(
+                current_arr, mesh_dim, [(dev, (dev + b) % state_next) for dev in range(state_next)]
+            )
+        )
+    all_rows = jnp.stack(vals, axis=0)[(vec_out - jnp.arange(state_next)) % state_next]
+    w1 = matrix_time(all_rows, in_array)
+    return w1
 
 
 def extended_2(cells, sides, width):
@@ -81,9 +112,7 @@
     conc_out = chemistry(moved, reaction)
     outgoing = jnp.zeros((bal_count * capacity, width), jnp.bfloat16).at[slot].set(conc_out)
     outgoing = outgoing.reshape(bal_count, capacity, width)
-    chem_slots = lax.all_to_all(outgoing, "bal", split_axis=0, concat_axis=0, tiled=True).reshape(
-        -1, width
-    )
+    chem_slots = run_convert(outgoing, "bal", 0, 0).reshape(-1, width)
     return (conc_out, chem_slots)
 
 

time: 135 us -> 130 us (0.963)
  the two profiles are of different devices: /device:TPU:0 before, /device:TPU:11 now
where the time goes in v1:
time: 130 us; the launch traced here: 129 us
  waiting for transfers between devices  53.1 us (41%)
  other arithmetic  44.6 us (34%)
  local copies, waits for them, and re-layouts  17.1 us (13%)
  starting transfers between devices  8.35 us (6%)
  matrix products  4.51 us (3%)
    ppermute x3, waiting for transfers between devices, run_convert(): lax.ppermute(current_arr, mesh_dim, [(dev, (dev + b) % state_next) for de...  21.3 us
    scatter-add x8, other arithmetic, shards(): sent = sent.at[ext_index[:, column]].add(flux)  20.9 us
    ppermute x1, waiting for transfers between devices, extended_2(): lax.ppermute(tail, axis, [(i, (i + 1) % count) for i in range(count)])  18.6 us
    gather x8, local copies, waits for them, and re-layouts, shards(): extended[ext_index[:, column]] - own_blocks  12.9 us
    ppermute x2, waiting for transfers between devices, shifted(): return lax.ppermute(value, axis, pairs)  11.6 us
    mul x1, other arithmetic, shards(): coefs[:, column][:, None, None]  7.75 us
    scatter x1, other arithmetic, shards(): jnp.zeros((bal_count * capacity, width), jnp.bfloat16).at[slot]  6.05 us
    ppermute x3, starting transfers between devices, run_convert(): lax.ppermute(current_arr, mesh_dim, [(dev, (dev + b) % state_next) for de...  3.83 us
  transfers between devices with their start and end apart: 7, of which 6 were waited for; matrix products, arithmetic and copies ran while one was open for 4% of the time, Pallas kernels for 0%

profile of v1, /device:TPU:11, one launch (start us, length us, event | category | flops | bytes accessed | tf_op | source)
XLA Modules:
  0.0 129.0 jit_solution(17770512866854425182)
XLA Ops:
  0.6 1.8 %collective-permute-start = (f32[16,128,128]{2,1,0:T(8,128)}, f32[16,128,128]{2,1,0:T(8,128)S(1)}, u32[]{:S(2)}, u32[]{:S(2)}) collective-permute-start(f32[16,128,128]{2,1,0:T(8,128)} %bitcast.81), channel_id=1, source_target_pairs={{0,4},{4,8},{8,12},{12,16},{16,20},{20,24},{24,28},{28,0},{1,5},{5... | collective-permute-start | bytes 3145736 | tf_op jit(solution)/shard_map/ppermute | solution.py:50
  2.5 0.7 fusion.19
  3.2 0.7 fusion.15
  3.9 1.1 reduce-window.6
  5.5 0.7 multiply_select_fusion
  6.3 18.6 %collective-permute-done = f32[16,128,128]{2,1,0:T(8,128)S(1)} collective-permute-done((f32[16,128,128]{2,1,0:T(8,128)}, f32[16,128,128]{2,1,0:T(8,128)S(1)}, u32[]{:S(2)}, u32[]{:S(2)}) %collective-permute-start) | collective-permute-done | bytes 1048608 | tf_op jit(solution)/shard_map/ppermute | solution.py:50
  24.9 1.0 copy-done.7
  25.9 1.5 %collective-permute-done.1 = f32[16,128,128]{2,1,0:T(8,128)} collective-permute-done((f32[16,128,128]{2,1,0:T(8,128)}, f32[16,128,128]{2,1,0:T(8,128)}, u32[]{:S(2)}, u32[]{:S(2)}) %collective-permute-start.1) | collective-permute-done | bytes 1048608 | tf_op jit(solution)/shard_map/ppermute | solution.py:52
  27.4 2.1 %pad_maximum_fusion = f32[48,128,128]{2,1,0:T(8,128)S(1)} fusion(f32[16,128,128]{2,1,0:T(8,128)} %collective-permute-done.1, f32[16,128,128]{2,1,0:T(8,128)} %bitcast.83, f32[16,128,128]{2,1,0:T(8,128)} %copy-done.7), kind=kLoop, calls=%fused_computation.22 | loop fusion | flops 1572864 | bytes 6291456 | tf_op jit(solution)/shard_map/concatenate | solution.py:48
  29.5 1.6 %gather_fusion = f32[16,128,128]{2,1,0:T(8,128)} fusion(f32[48,128,128]{2,1,0:T(8,128)S(1)} %pad_maximum_fusion, s32[1024]{0:T(1024)S(1)} %get-tuple-element.63), kind=kCustom, calls=%fused_computation | custom fusion | bytes 2097216 | tf_op jit(solution)/shard_map/gather | solution.py:95
  31.1 1.6 %gather_fusion.1 = f32[16,128,128]{2,1,0:T(8,128)} fusion(f32[48,128,128]{2,1,0:T(8,128)S(1)} %pad_maximum_fusion, s32[1024]{0:T(1024)S(1)} %get-tuple-element.62), kind=kCustom, calls=%fused_computation.1 | custom fusion | bytes 2097216 | tf_op jit(solution)/shard_map/gather | solution.py:95
  32.7 1.6 %gather_fusion.2 = f32[16,128,128]{2,1,0:T(8,128)} fusion(f32[48,128,128]{2,1,0:T(8,128)S(1)} %pad_maximum_fusion, s32[1024]{0:T(1024)S(1)} %get-tuple-element.61), kind=kCustom, calls=%fused_computation.2 | custom fusion | bytes 2097216 | tf_op jit(solution)/shard_map/gather | solution.py:95
  34.3 1.6 %gather_fusion.3 = f32[16,128,128]{2,1,0:T(8,128)} fusion(f32[48,128,128]{2,1,0:T(8,128)S(1)} %pad_maximum_fusion, s32[1024]{0:T(1024)S(1)} %get-tuple-element.60), kind=kCustom, calls=%fused_computation.3 | custom fusion | bytes 2097216 | tf_op jit(solution)/shard_map/gather | solution.py:95
  35.9 1.6 %gather_fusion.4 = f32[16,128,128]{2,1,0:T(8,128)} fusion(f32[48,128,128]{2,1,0:T(8,128)S(1)} %pad_maximum_fusion, s32[1024]{0:T(1024)S(1)} %get-tuple-element.59), kind=kCustom, calls=%fused_computation.4 | custom fusion | bytes 2097216 | tf_op jit(solution)/shard_map/gather | solution.py:95
  37.5 1.6 %gather_fusion.5 = f32[16,128,128]{2,1,0:T(8,128)} fusion(f32[48,128,128]{2,1,0:T(8,128)S(1)} %pad_maximum_fusion, s32[1024]{0:T(1024)S(1)} %get-tuple-element.58), kind=kCustom, calls=%fused_computation.5 | custom fusion | bytes 2097216 | tf_op jit(solution)/shard_map/gather | solution.py:95
  39.1 1.6 %gather_fusion.6 = f32[16,128,128]{2,1,0:T(8,128)} fusion(f32[48,128,128]{2,1,0:T(8,128)S(1)} %pad_maximum_fusion, s32[1024]{0:T(1024)S(1)} %get-tuple-element.57), kind=kCustom, calls=%fused_computation.6 | custom fusion | bytes 2097216 | tf_op jit(solution)/shard_map/gather | solution.py:95
  40.8 1.6 %gather_fusion.7 = f32[16,128,128]{2,1,0:T(8,128)} fusion(f32[48,128,128]{2,1,0:T(8,128)S(1)} %pad_maximum_fusion, s32[1024]{0:T(1024)S(1)} %get-tuple-element.56), kind=kCustom, calls=%fused_computation.7 | custom fusion | bytes 2097216 | tf_op jit(solution)/shard_map/gather | solution.py:95
  42.3 7.7 %subtract_multiply_fusion = (f32[16,128,128]{2,1,0:T(8,128)}, f32[16,128,128]{2,1,0:T(8,128)}, f32[16,128,128]{2,1,0:T(8,128)}, f32[16,128,128]{2,1,0:T(8,128)},...) fusion(f32[16,128,128]{2,1,0:T(8,128)} %gather_fusion.7, ...), kind=kLoop, calls=%fused_computation.33 | loop fusion | flops 4194304 | bytes 17826304 | tf_op jit(solution)/shard_map/mul | solution.py:95
  50.1 0.4 broadcast_in_dim.15
  50.5 2.6 %scatter_fusion = f32[48,128,128]{2,1,0:T(8,128)S(1)} fusion(f32[48,128,128]{2,1,0:T(8,128)S(1)} %broadcast_in_dim.15, s32[16]{0:T(128)S(1)} %get-tuple-element.55, f32[16,128,128]{2,1,0:T(8,128)} %get-tuple-element.39), kind=kCustom, calls=%fused_computation.9 | custom fusion | flops 262144 | bytes 3145792 | tf_op jit(solution)/shard_map/scatter-add | solution.py:97
  53.1 2.6 %scatter_fusion.1 = f32[48,128,128]{2,1,0:T(8,128)S(1)} fusion(f32[48,128,128]{2,1,0:T(8,128)S(1)} %scatter_fusion, s32[16]{0:T(128)S(1)} %get-tuple-element.54, f32[16,128,128]{2,1,0:T(8,128)} %get-tuple-element.38), kind=kCustom, calls=%fused_computation.10 | custom fusion | flops 262144 | bytes 3145792 | tf_op jit(solution)/shard_map/scatter-add | solution.py:97
  55.7 2.6 %scatter_fusion.2 = f32[48,128,128]{2,1,0:T(8,128)S(1)} fusion(f32[48,128,128]{2,1,0:T(8,128)S(1)} %scatter_fusion.1, s32[16]{0:T(128)S(1)} %get-tuple-element.53, f32[16,128,128]{2,1,0:T(8,128)} %get-tuple-element.37), kind=kCustom, calls=%fused_computation.11 | custom fusion | flops 262144 | bytes 3145792 | tf_op jit(solution)/shard_map/scatter-add | solution.py:97
  58.3 2.6 %scatter_fusion.3 = f32[48,128,128]{2,1,0:T(8,128)S(1)} fusion(f32[48,128,128]{2,1,0:T(8,128)S(1)} %scatter_fusion.2, s32[16]{0:T(128)S(1)} %get-tuple-element.52, f32[16,128,128]{2,1,0:T(8,128)} %get-tuple-element.36), kind=kCustom, calls=%fused_computation.12 | custom fusion | flops 262144 | bytes 3145792 | tf_op jit(solution)/shard_map/scatter-add | solution.py:97
  60.9 2.6 %scatter_fusion.4 = f32[48,128,128]{2,1,0:T(8,128)S(1)} fusion(f32[48,128,128]{2,1,0:T(8,128)S(1)} %scatter_fusion.3, s32[16]{0:T(128)S(1)} %get-tuple-element.51, f32[16,128,128]{2,1,0:T(8,128)} %get-tuple-element.35), kind=kCustom, calls=%fused_computation.13 | custom fusion | flops 262144 | bytes 3145792 | tf_op jit(solution)/shard_map/scatter-add | solution.py:97
  63.5 2.6 %scatter_fusion.5 = f32[48,128,128]{2,1,0:T(8,128)S(1)} fusion(f32[48,128,128]{2,1,0:T(8,128)S(1)} %scatter_fusion.4, s32[16]{0:T(128)S(1)} %get-tuple-element.50, f32[16,128,128]{2,1,0:T(8,128)} %get-tuple-element.34), kind=kCustom, calls=%fused_computation.14 | custom fusion | flops 262144 | bytes 3145792 | tf_op jit(solution)/shard_map/scatter-add | solution.py:97
  66.1 2.6 %scatter_fusion.6 = f32[48,128,128]{2,1,0:T(8,128)S(1)} fusion(f32[48,128,128]{2,1,0:T(8,128)S(1)} %scatter_fusion.5, s32[16]{0:T(128)S(1)} %get-tuple-element.49, f32[16,128,128]{2,1,0:T(8,128)} %get-tuple-element.33), kind=kCustom, calls=%fused_computation.15 | custom fusion | flops 262144 | bytes 3145792 | tf_op jit(solution)/shard_map/scatter-add | solution.py:97
  68.8 2.6 %scatter_fusion.7 = f32[48,128,128]{2,1,0:T(8,128)S(1)} fusion(f32[48,128,128]{2,1,0:T(8,128)S(1)} %scatter_fusion.6, s32[16]{0:T(128)S(1)} %get-tuple-element.48, f32[16,128,128]{2,1,0:T(8,128)} %get-tuple-element.32), kind=kCustom, calls=%fused_computation.16 | custom fusion | flops 262144 | bytes 3145792 | tf_op jit(solution)/shard_map/scatter-add | solution.py:97
  71.9 2.6 %collective-permute-start.3 = (bf16[16,128,128]{2,1,0:T(8,128)(2,1)S(1)}, bf16[16,128,128]{2,1,0:T(8,128)(2,1)S(1)}, u32[]{:S(2)}, u32[]{:S(2)}) collective-permute-start(bf16[16,128,128]{2,1,0:T(8,128)(2,1)S(1)} %get-tuple-element.27), channel_id=1, source_target_pairs={{0,4},{4,8},{8,12},{12,16},{16,20},{20,24},{24,28},{28,0},{1,5},{5... | collective-permute-start | bytes 1572872 | tf_op jit(solution)/shard_map/ppermute | solution.py:62
  74.6 11.6 %collective-permute-done.2 = bf16[16,128,128]{2,1,0:T(8,128)(2,1)S(1)} collective-permute-done((bf16[16,128,128]{2,1,0:T(8,128)(2,1)S(1)}, bf16[16,128,128]{2,1,0:T(8,128)(2,1)S(1)}, u32[]{:S(2)}, u32[]{:S(2)}) %collective-permute-start.2) | collective-permute-done | bytes 524320 | tf_op jit(solution)/shard_map/ppermute | solution.py:62
  86.2 3.1 %fusion.6 = f32[16,128,128]{2,1,0:T(8,128)S(1)} fusion(f32[16,128,128]{2,1,0:T(8,128)} %bitcast.85, f32[48,128,128]{2,1,0:T(8,128)S(1)} %scatter_fusion.7, bf16[16,128,128]{2,1,0:T(8,128)(2,1)S(1)} %collective-permute-done.3, bf16[16,128,128]{2,1,0:T(8,128)(2,1)S(1)} %collective-permute-done.2, f32[16,128,128]{2,1,0:T(8,128)S(1)} %copy-done.1, ...), kind=kLoop, calls=%fused_computation.28 | loop fusion | flops 3407872 | bytes 12582912 | tf_op jit(solution)/shard_map/add | solution.py:101
  89.3 1.1 fusion.8
  90.4 4.7 %while.10 = (s32[]{:T(128)}, f32[2048,128]{1,0:T(8,128)S(1)}, bf16[128,128]{1,0:T(8,128)(2,1)S(1)}, s32[]{:T(128)}) while((s32[]{:T(128)}, f32[2048,128]{1,0:T(8,128)S(1)}, bf16[128,128]{1,0:T(8,128)(2,1)S(1)}, s32[]{:T(128)}) %tuple.54), condition=%wide.region_9.10_spmd, body=%wide.region_8.9_spmd.sunk | while | flops 67895296 | bytes 4227125 | solution.py:73
  90.5 0.3 fusion.40
  91.2 0.3 fusion.40
  91.6 0.3 fusion.40
  92.4 0.3 fusion.40
  93.6 0.3 fusion.40
  94.0 0.3 fusion.40
  94.7 0.3 fusion.40
  95.0 6.0 %scatter_custom_fusion.8 = bf16[4096,128]{1,0:T(8,128)(2,1)S(1)} fusion(s32[2048]{0:T(1024)S(1)} %bitcast.94, bf16[]{:T(256)} %constant.106.clone.1, f32[2048,128]{1,0:T(8,128)S(1)} %get-tuple-element.19), kind=kCustom, calls=%fused_computation.42 | custom fusion | flops 262144 | bytes 2097154 | tf_op jit(solution)/shard_map/scatter | solution.py:113
  101.2 1.3 %collective-permute-start.4 = (bf16[1,1024,128]{2,1,0:T(8,128)(2,1)S(1)}, bf16[1,1024,128]{2,1,0:T(8,128)(2,1)S(1)}, u32[]{:S(2)}, u32[]{:S(2)}) collective-permute-start(bf16[1,1024,128]{2,1,0:T(8,128)(2,1)S(1)} %get-tuple-element.31), channel_id=1, source_target_pairs={{0,1},{1,2},{2,3},{3,0},{4,5},{5,6},{6,7},{7,4},{8,9},{9,10},{10,1... | collective-permute-start | bytes 786440 | tf_op jit(solution)/shard_map/ppermute | solution.py:34
  102.5 1.1 collective-permute-start.5
  103.6 1.4 %collective-permute-start.6 = (bf16[1,1024,128]{2,1,0:T(8,128)(2,1)S(1)}, bf16[1,1024,128]{2,1,0:T(8,128)(2,1)S(1)}, u32[]{:S(2)}, u32[]{:S(2)}) collective-permute-start(bf16[1,1024,128]{2,1,0:T(8,128)(2,1)S(1)} %get-tuple-element.29), channel_id=1, source_target_pairs={{0,3},{1,0},{2,1},{3,2},{4,7},{5,4},{6,5},{7,6},{8,11},{9,8},{10,9... | collective-permute-start | bytes 786440 | tf_op jit(solution)/shard_map/ppermute | solution.py:34
  105.0 0.8 convert_element_type.36
  105.9 2.7 %collective-permute-done.4 = bf16[1,1024,128]{2,1,0:T(8,128)(2,1)S(1)} collective-permute-done((bf16[1,1024,128]{2,1,0:T(8,128)(2,1)S(1)}, bf16[1,1024,128]{2,1,0:T(8,128)(2,1)S(1)}, u32[]{:S(2)}, u32[]{:S(2)}) %collective-permute-start.4) | collective-permute-done | bytes 262176 | tf_op jit(solution)/shard_map/ppermute | solution.py:34
  108.6 15.9 %collective-permute-done.5 = bf16[1,1024,128]{2,1,0:T(8,128)(2,1)S(1)} collective-permute-done((bf16[1,1024,128]{2,1,0:T(8,128)(2,1)S(1)}, bf16[1,1024,128]{2,1,0:T(8,128)(2,1)S(1)}, u32[]{:S(2)}, u32[]{:S(2)}) %collective-permute-start.5) | collective-permute-done | bytes 262176 | tf_op jit(solution)/shard_map/ppermute | solution.py:34
  124.5 2.7 %collective-permute-done.6 = bf16[1,1024,128]{2,1,0:T(8,128)(2,1)S(1)} collective-permute-done((bf16[1,1024,128]{2,1,0:T(8,128)(2,1)S(1)}, bf16[1,1024,128]{2,1,0:T(8,128)(2,1)S(1)}, u32[]{:S(2)}, u32[]{:S(2)}) %collective-permute-start.6) | collective-permute-done | bytes 262176 | tf_op jit(solution)/shard_map/ppermute | solution.py:34
  127.4 1.7 %gather_fusion.8 = bf16[4,1024,128]{2,1,0:T(8,128)(2,1)} fusion(bf16[4,1024,128]{2,1,0:T(8,128)(2,1)S(1)} %maximum_bitcast_fusion, s32[1024]{0:T(1024)S(1)} %pad_clamp_fusion), kind=kCustom, calls=%fused_computation.8 | custom fusion | bytes 2097168 | tf_op jit(solution)/shard_map/gather | solution.py:38
  (58 shorter events, 3.5 us)
Async XLA Ops:
  0.6 88.7 %copy-start = (f32[32,128]{1,0:T(8,128)S(1)}, f32[32,128]{1,0:T(8,128)}, u32[]{:S(2)}) copy-start(f32[32,128]{1,0:T(8,128)} %param.16) | copy-start | bytes 49156
  0.6 24.3 %collective-permute-start = (f32[16,128,128]{2,1,0:T(8,128)}, f32[16,128,128]{2,1,0:T(8,128)S(1)}, u32[]{:S(2)}, u32[]{:S(2)}) collective-permute-start(f32[16,128,128]{2,1,0:T(8,128)} %bitcast.81), channel_id=1, source_target_pairs={{0,4},{4,8},{8,12},{12,16},{16,20},{20,24},{24,28},{28,0},{1,5},{5... | collective-permute-start | bytes 3145736 | tf_op jit(solution)/shard_map/ppermute | solution.py:50
  2.5 24.9 %collective-permute-start.1 = (f32[16,128,128]{2,1,0:T(8,128)}, f32[16,128,128]{2,1,0:T(8,128)}, u32[]{:S(2)}, u32[]{:S(2)}) collective-permute-start(f32[16,128,128]{2,1,0:T(8,128)} %bitcast.82), channel_id=1, source_target_pairs={{4,0},{8,4},{12,8},{16,12},{20,16},{24,20},{28,24},{0,28},{5,1},{9... | collective-permute-start | bytes 3145736 | tf_op jit(solution)/shard_map/ppermute | solution.py:52
  24.9 1.0 copy-start.7
  71.4 3.1 %copy-start.9 = (s32[2048,1]{0,1:T(1,128)S(1)}, s32[2048,1]{0,1:T(1,128)}, u32[]{:S(2)}) copy-start(s32[2048,1]{0,1:T(1,128)} %param.15) | copy-start | bytes 24580
  71.4 14.8 %copy-start.1 = (f32[16,128,128]{2,1,0:T(8,128)S(1)}, f32[16,128,128]{2,1,0:T(8,128)}, u32[]{:S(2)}) copy-start(f32[16,128,128]{2,1,0:T(8,128)} %get-tuple-element.32) | copy-start | bytes 3145732
  71.4 14.8 %copy-start.2 = (f32[16,128,128]{2,1,0:T(8,128)S(1)}, f32[16,128,128]{2,1,0:T(8,128)}, u32[]{:S(2)}) copy-start(f32[16,128,128]{2,1,0:T(8,128)} %get-tuple-element.33) | copy-start | bytes 3145732
  71.4 14.8 %copy-start.3 = (f32[16,128,128]{2,1,0:T(8,128)S(1)}, f32[16,128,128]{2,1,0:T(8,128)}, u32[]{:S(2)}) copy-start(f32[16,128,128]{2,1,0:T(8,128)} %get-tuple-element.34) | copy-start | bytes 3145732
  71.4 14.8 %copy-start.4 = (f32[16,128,128]{2,1,0:T(8,128)S(1)}, f32[16,128,128]{2,1,0:T(8,128)}, u32[]{:S(2)}) copy-start(f32[16,128,128]{2,1,0:T(8,128)} %get-tuple-element.35) | copy-start | bytes 3145732
  71.4 14.8 %copy-start.5 = (f32[16,128,128]{2,1,0:T(8,128)S(1)}, f32[16,128,128]{2,1,0:T(8,128)}, u32[]{:S(2)}) copy-start(f32[16,128,128]{2,1,0:T(8,128)} %get-tuple-element.36) | copy-start | bytes 3145732
  71.4 14.8 %copy-start.6 = (f32[16,128,128]{2,1,0:T(8,128)S(1)}, f32[16,128,128]{2,1,0:T(8,128)}, u32[]{:S(2)}) copy-start(f32[16,128,128]{2,1,0:T(8,128)} %get-tuple-element.37) | copy-start | bytes 3145732
  71.8 14.4 %collective-permute-start.2 = (bf16[16,128,128]{2,1,0:T(8,128)(2,1)S(1)}, bf16[16,128,128]{2,1,0:T(8,128)(2,1)S(1)}, u32[]{:S(2)}, u32[]{:S(2)}) collective-permute-start(bf16[16,128,128]{2,1,0:T(8,128)(2,1)S(1)} %get-tuple-element.26), channel_id=1, source_target_pairs={{0,28},{4,0},{8,4},{12,8},{16,12},{20,16},{24,20},{28,24},{1,29},{... | collective-permute-start | bytes 1572872 | tf_op jit(solution)/shard_map/ppermute | solution.py:62
  71.9 14.3 %collective-permute-start.3 = (bf16[16,128,128]{2,1,0:T(8,128)(2,1)S(1)}, bf16[16,128,128]{2,1,0:T(8,128)(2,1)S(1)}, u32[]{:S(2)}, u32[]{:S(2)}) collective-permute-start(bf16[16,128,128]{2,1,0:T(8,128)(2,1)S(1)} %get-tuple-element.27), channel_id=1, source_target_pairs={{0,4},{4,8},{8,12},{12,16},{16,20},{20,24},{24,28},{28,0},{1,5},{5... | collective-permute-start | bytes 1572872 | tf_op jit(solution)/shard_map/ppermute | solution.py:62
  74.6 14.7 %copy-start.10 = (s32[2048]{0:T(1024)S(1)}, s32[2048]{0:T(1024)}, u32[]{:S(2)}) copy-start(s32[2048]{0:T(1024)} %param.14) | copy-start | bytes 24580
  74.6 15.8 %copy-start.8 = (bf16[128,128]{1,0:T(8,128)(2,1)S(1)}, bf16[128,128]{1,0:T(8,128)(2,1)}, u32[]{:S(2)}) copy-start(bf16[128,128]{1,0:T(8,128)(2,1)} %param.17) | copy-start | bytes 98308
  101.2 7.4 %collective-permute-start.4 = (bf16[1,1024,128]{2,1,0:T(8,128)(2,1)S(1)}, bf16[1,1024,128]{2,1,0:T(8,128)(2,1)S(1)}, u32[]{:S(2)}, u32[]{:S(2)}) collective-permute-start(bf16[1,1024,128]{2,1,0:T(8,128)(2,1)S(1)} %get-tuple-element.31), channel_id=1, source_target_pairs={{0,1},{1,2},{2,3},{3,0},{4,5},{5,6},{6,7},{7,4},{8,9},{9,10},{10,1... | collective-permute-start | bytes 786440 | tf_op jit(solution)/shard_map/ppermute | solution.py:34
  102.5 22.0 %collective-permute-start.5 = (bf16[1,1024,128]{2,1,0:T(8,128)(2,1)S(1)}, bf16[1,1024,128]{2,1,0:T(8,128)(2,1)S(1)}, u32[]{:S(2)}, u32[]{:S(2)}) collective-permute-start(bf16[1,1024,128]{2,1,0:T(8,128)(2,1)S(1)} %get-tuple-element.30), channel_id=1, source_target_pairs={{0,2},{1,3},{2,0},{3,1},{4,6},{5,7},{6,4},{7,5},{8,10},{9,11},{10,... | collective-permute-start | bytes 786440 | tf_op jit(solution)/shard_map/ppermute | solution.py:34
  103.6 23.6 %collective-permute-start.6 = (bf16[1,1024,128]{2,1,0:T(8,128)(2,1)S(1)}, bf16[1,1024,128]{2,1,0:T(8,128)(2,1)S(1)}, u32[]{:S(2)}, u32[]{:S(2)}) collective-permute-start(bf16[1,1024,128]{2,1,0:T(8,128)(2,1)S(1)} %get-tuple-element.29), channel_id=1, source_target_pairs={{0,3},{1,0},{2,1},{3,2},{4,7},{5,4},{6,5},{7,6},{8,11},{9,8},{10,9... | collective-permute-start | bytes 786440 | tf_op jit(solution)/shard_map/ppermute | solution.py:34
